TPU v7x, 256 devices: a whole 4x4x8 slice. The times are simulated.
256 devices in a mesh: mem: 32 (over z, x), lon: 4 (over y), lat: 2 (over core).
Axes of the slice: x: 4, y: 4, z: 8, core: 2. Of those that a mesh axis runs over, the one named last changes fastest.
Arguments:
- ens_obs: bfloat16 [1024, 8, 16, 128], P('mem', 'lat', 'lon'), may hold values from -16 to 16
- innovation: bfloat16 [8, 16, 128], P('lat', 'lon'), may hold values from -6 to 6
- obs_weight: bfloat16 [8, 16, 128], P('lat', 'lon'), may hold values from 0.5 to 5
- loc_list: int32 [32, 8, 4], P(None, ('lon', 'lat')), may hold values from 0 to 47, as said below
- counts: int32 [32, 8], P('mem', ('lon', 'lat')), may hold values from 1 to 4, as said below
- taper: float32 [32, 8, 4], P('mem', ('lon', 'lat')), may hold values from 0.2 to 1
- state: bfloat16 [1024, 32, 8, 1280], P('mem', None, ('lon', 'lat')), may hold values from -6 to 6
Outputs:
- analysis: bfloat16 [1024, 32, 8, 1280], P('mem', None, ('lon', 'lat'))
Inputs may be any that keep to these rules, and one draw needn't show every extreme that they name: `loc_list`: the 4 entries of a patch name different window blocks; only the first counts entries are used. `counts`: some patch uses all 4 listed blocks in every draw.
All inputs are finite; a program needn't handle non-finite values.
Results may differ from a plain program's by a relative error of at most 0.0068.
Values may be sent and summed in bfloat16 or wider, within the bound.
A program may use at most 64 MiB of HBM per device.

v0:
```python
import jax
import jax.numpy as jnp
from jax import lax
from jax.sharding import PartitionSpec as P

NSI = 2


def padded(block, sides, width):
    for axis, dim in sides:
        count = lax.axis_size(axis)
        forward = [(i, i + 1) for i in range(count - 1)]
        forward.append((count - 1, 0))
        backward = [(target, source) for source, target in forward]
        low = lax.ppermute(
            lax.slice_in_dim(block, block.shape[dim] - width, None, axis=dim), axis, forward
        )
        high = lax.ppermute(lax.slice_in_dim(block, 0, width, axis=dim), axis, backward)
        block = jnp.concatenate([low, block, high], axis=dim)
    return block


def inverse_root(start_low):
    member_total = start_low.shape[0]
    identity = jnp.eye(member_total, dtype=jnp.float32)
    upper_iter = start_low
    lower_iter = start_low
    for sweep_index in range(NSI):
        if sweep_index == 0:
            product = start_low.astype(jnp.float32)
        else:
            product = jnp.dot(lower_iter, upper_iter, preferred_element_type=jnp.float32)
        halfstep = 0.5 * (3.0 * identity - product)
        half_low = halfstep.astype(jnp.bfloat16)
        if sweep_index == NSI - 1:
            return jnp.dot(half_low, lower_iter, preferred_element_type=jnp.float32)
        next_upper = jnp.dot(upper_iter, half_low, preferred_element_type=jnp.float32).astype(
            jnp.bfloat16
        )
        lower_iter = half_low
        upper_iter = next_upper


def weights_from_gram(gram_mat, drive_vec):
    member_total = gram_mat.shape[0]
    divisor = float(member_total - 1)
    identity = jnp.eye(member_total, dtype=jnp.float32)
    a_matrix = identity + gram_mat / divisor
    trace_level = 2.0 * jnp.trace(a_matrix) / member_total
    start_low = lax.optimization_barrier((a_matrix / trace_level).astype(jnp.bfloat16))
    inv_root = (inverse_root(start_low) / jnp.sqrt(trace_level)).astype(jnp.bfloat16)
    inner_vec = jnp.dot(
        inv_root, (drive_vec / divisor).astype(jnp.bfloat16), preferred_element_type=jnp.float32
    )
    mean_weights = jnp.dot(
        inv_root, inner_vec.astype(jnp.bfloat16), preferred_element_type=jnp.float32
    )
    return (inv_root.astype(jnp.float32) + mean_weights[:, None]).astype(jnp.bfloat16)


def on_device(ens_obs, innovation, obs_weight, loc_list, counts, taper, state):
    local_members, band_rows, band_cols, block_len = ens_obs.shape
    group_patches = loc_list.shape[0]
    slot_count = loc_list.shape[2]
    own_count = taper.shape[0]
    state_len = state.shape[3]
    stacked = jnp.concatenate([ens_obs, innovation[None], obs_weight[None]], axis=0)
    framed = padded(stacked, (("lon", 2),), band_cols)
    window = framed.reshape(local_members + 2, band_rows * 3 * band_cols, block_len)
    picked = window[:, loc_list[:, 0, :], :]
    ens_part = picked[:local_members].reshape(local_members, group_patches, slot_count * block_len)
    first_slot = lax.axis_index("mem") * own_count
    own_side = jnp.moveaxis(
        lax.dynamic_slice_in_dim(picked[local_members:], first_slot, own_count, 1), 1, 0
    )
    flat_state = state.reshape(local_members, group_patches, state_len)
    ens_full = lax.all_to_all(ens_part, "mem", split_axis=1, concat_axis=0, tiled=True)

    def patch_weights(inputs):
        patch_index, tapers, live_count, obs_side = inputs
        selected = lax.dynamic_index_in_dim(ens_full, patch_index, 1, keepdims=False)
        live_mask = (jnp.arange(slot_count, dtype=jnp.int32) < live_count).astype(jnp.float32)
        obs_factor = obs_side[1].astype(jnp.float32) * (tapers * live_mask)[:, None]
        weighted = (selected * obs_factor.reshape(-1)).astype(jnp.bfloat16)
        gram_mat = lax.dot_general(
            weighted, selected, (((1,), (1,)), ((), ())), preferred_element_type=jnp.float32
        )
        drive_vec = jnp.dot(weighted, obs_side[0].reshape(-1), preferred_element_type=jnp.float32)
        return weights_from_gram(gram_mat, drive_vec)

    weight_stack = lax.map(
        patch_weights,
        (jnp.arange(own_count, dtype=jnp.int32), taper[:, 0, :], counts[:, 0], own_side),
    )
    state_full = lax.all_to_all(flat_state, "mem", split_axis=1, concat_axis=0, tiled=True)
    analysis_own = jnp.einsum(
        "pkj,kps->jps", weight_stack, state_full, preferred_element_type=jnp.float32
    ).astype(jnp.bfloat16)
    returned = lax.all_to_all(analysis_own, "mem", split_axis=0, concat_axis=1, tiled=True)
    return returned.reshape(local_members, group_patches, 1, state_len)


def solution(mesh):
    return jax.shard_map(
        on_device,
        mesh=mesh,
        in_specs=(
            P("mem", "lat", "lon", None),
            P("lat", "lon", None),
            P("lat", "lon", None),
            P(None, ("lon", "lat"), None),
            P("mem", ("lon", "lat")),
            P("mem", ("lon", "lat"), None),
            P("mem", None, ("lon", "lat"), None),
        ),
        out_specs=P("mem", None, ("lon", "lat"), None),
        check_vma=False,
    )
```

profile of v0, /device:TPU:32, one launch (start us, length us, event | category | flops | bytes accessed | tf_op | source)
XLA Modules:
  0.0 211.7 jit_solution(16215918792205847067)
XLA Ops:
  0.0 1.0 pad_maximum_fusion.1
  1.0 3.1 %collective-permute-start.1 = (bf16[34,4,4,128]{3,2,1,0:T(4,128)(2,1)S(1)}, bf16[34,4,4,128]{3,2,1,0:T(4,128)(2,1)S(1)}, u32[]{:S(2)}, u32[]{:S(2)}) collective-permute-start(bf16[34,4,4,128]{3,2,1,0:T(4,128)(2,1)S(1)} %pad_maximum_fusion.1), channel_id=1, source_target_pairs={{2,0},{4,2},{6,4},{0,6},{3,1},{5,3},{7,5},{1,7},{10,8},{12,10},{14... | collective-permute-start | bytes 417800 | tf_op jit(solution)/shard_map/ppermute | solution.py:18
  4.1 0.7 compare_select_fusion
  5.0 2.0 collective-permute-done.1
  7.1 3.4 %collective-permute-done = bf16[34,4,4,128]{3,2,1,0:T(4,128)(2,1)S(1)} collective-permute-done((bf16[34,4,4,128]{3,2,1,0:T(4,128)(2,1)S(1)}, bf16[34,4,4,128]{3,2,1,0:T(4,128)(2,1)S(1)}, u32[]{:S(2)}, u32[]{:S(2)}) %collective-permute-start) | collective-permute-done | bytes 139296 | tf_op jit(solution)/shard_map/ppermute | solution.py:15
  10.5 1.2 pad_maximum_fusion
  12.0 0.8 gather_fusion
  12.8 0.6 copy.40
  13.4 0.6 slice.22
  14.1 0.4 reshape.115
  14.5 1.5 copy.35
  16.1 11.2 %all-to-all-start = ((bf16[32,32,512]{2,0,1:T(8,128)(2,1)}), bf16[32,32,512]{2,0,1:T(8,128)(2,1)S(1)}, u32[]{:S(2)}, u32[]{:S(2)}) async-start(bf16[32,32,512]{2,0,1:T(8,128)(2,1)} %copy.35), calls=%async_computation | async-start | bytes 2097152 | tf_op jit(solution)/shard_map/all_to_all | solution.py:77
  27.3 4.7 %copy.39 = bf16[32,32,1,1280]{3,0,1,2:T(8,128)(2,1)} copy(bf16[32,32,1,1280]{3,1,2,0:T(8,128)(2,1)} %param.13) | data formatting | bytes 5242880 | tf_op args[6]
  31.9 21.7 %all-to-all-done = bf16[32,32,512]{2,0,1:T(8,128)(2,1)S(1)} async-done(((bf16[32,32,512]{2,0,1:T(8,128)(2,1)}), bf16[32,32,512]{2,0,1:T(8,128)(2,1)S(1)}, u32[]{:S(2)}, u32[]{:S(2)}) %all-to-all-start) | async-done | bytes 1048608 | tf_op jit(solution)/shard_map/all_to_all | solution.py:77
  53.6 6.3 %all-to-all-start.1 = ((bf16[32,32,1280]{2,0,1:T(8,128)(2,1)}), bf16[32,32,1280]{2,0,1:T(8,128)(2,1)}, u32[]{:S(2)}, u32[]{:S(2)}) async-start(bf16[32,32,1280]{2,0,1:T(8,128)(2,1)} %bitcast.59), calls=%async_computation.1 | async-start | bytes 5242880 | tf_op jit(solution)/shard_map/all_to_all | solution.py:95
  60.9 0.4 fusion.32
  61.3 3.8 %select_reduce_fusion = (f32[]{:T(128)}, f32[1024,1024]{1,0:T(8,128)}) fusion(bf16[1024,512]{1,0:T(8,128)(2,1)S(1)} %bitcast.69, bf16[1024,512]{1,0:T(8,128)(2,1)S(1)} %bitcast.67), kind=kOutput, calls=%fused_computation.10 | convolution fusion | flops 1080033280 | bytes 6291460 | tf_op jit(solution)/shard_map/while/body/eval_jaxpr/dot_general | solution.py:85
  65.8 2.8 %divide_convert_fusion.1 = bf16[1024,1024]{1,0:T(8,128)(2,1)S(1)} fusion(f32[1024,1024]{1,0:T(8,128)} %get-tuple-element.16, f32[]{:T(128)S(6)} %div.29), kind=kLoop, calls=%fused_computation.9 | loop fusion | flops 6291456 | bytes 6291460 | tf_op jit(solution)/shard_map/while/body/eval_jaxpr/convert_element_type | solution.py:50
  68.6 1.3 copy-done
  69.9 3.7 %fusion.21 = bf16[1024,1024]{1,0:T(8,128)(2,1)} fusion(bf16[1024,1024]{1,0:T(8,128)(2,1)S(1)} %divide_convert_fusion.1), kind=kOutput, calls=%fused_computation.24 | convolution fusion | flops 2153775104 | bytes 4194304 | tf_op jit(solution)/shard_map/while/body/eval_jaxpr/dot_general | solution.py:37
  73.6 7.4 %divide_convert_fusion = bf16[1024,1024]{1,0:T(8,128)(2,1)S(1)} fusion(f32[]{:T(128)S(6)} %sqrt.4, bf16[1024,1024]{1,0:T(8,128)(2,1)} %fusion.21, bf16[1024,1024]{1,0:T(8,128)(2,1)} %copy-done), kind=kOutput, calls=%fused_computation.8 | convolution fusion | flops 4314890240 | bytes 6291460 | tf_op jit(solution)/shard_map/while/body/eval_jaxpr/dot_general | solution.py:36
  81.0 0.6 fusion.33
  81.7 0.6 fusion.34
  82.3 37.0 %all-to-all-done.1 = bf16[32,32,1280]{2,0,1:T(8,128)(2,1)} async-done(((bf16[32,32,1280]{2,0,1:T(8,128)(2,1)}), bf16[32,32,1280]{2,0,1:T(8,128)(2,1)}, u32[]{:S(2)}, u32[]{:S(2)}) %all-to-all-start.1) | async-done | bytes 2621472 | tf_op jit(solution)/shard_map/all_to_all | solution.py:95
  119.3 6.1 %fusion.4 = bf16[1024,1,1280]{2,0,1:T(8,128)(2,1)} fusion(bf16[1024,1280]{1,0:T(8,128)(2,1)} %bitcast.22, bf16[1024,1024]{1,0:T(8,128)(2,1)S(1)} %divide_convert_fusion, f32[1024]{0:T(1024)S(1)} %bitcast.76), kind=kOutput, calls=%fused_computation.14 | convolution fusion | flops 2688811008 | bytes 7344128 | tf_op jit(solution)/shard_map/pkj,kps->jps/dot_general | solution.py:96
  125.4 0.5 broadcast.106
  126.0 4.4 %reduce = bf16[1024,1280]{1,0:T(8,128)(2,1)S(1)} reduce(bf16[1024,1,1280]{2,0,1:T(8,128)(2,1)} %fusion.4, bf16[]{:T(256)} %broadcast.106), dimensions={1}, to_apply=%copy.33.reduce_sub_computation | reduce | bytes 5242882 | tf_op jit(solution)/shard_map/convert_element_type | solution.py:98
  130.4 2.2 %reshape.116 = bf16[32,2,20480]{2,1,0:T(2,128)(2,1)} reshape(bf16[1024,1280]{1,0:T(8,128)(2,1)S(1)} %reduce) | data formatting | bytes 5242880
  132.6 66.1 %all_to_all.45 = bf16[32,2,20480]{2,1,0:T(2,128)(2,1)S(1)} all-to-all(bf16[32,2,20480]{2,1,0:T(2,128)(2,1)} %reshape.116), channel_id=1, replica_groups=mesh['mem'=32,'lon'=4,'lat'=2] {'mem'}, dimensions={0} | all-to-all | bytes 5242880 | tf_op jit(solution)/shard_map/all_to_all | solution.py:99
  198.7 7.2 %reshape.117 = bf16[1024,1,1280]{2,1,0:T(2,128)(2,1)} reshape(bf16[32,2,20480]{2,1,0:T(2,128)(2,1)S(1)} %all_to_all.45) | data formatting | bytes 5242880
  205.9 2.9 %copy.36 = bf16[1024,1,1280]{2,0,1:T(8,128)(2,1)S(1)} copy(bf16[1024,1,1280]{2,1,0:T(2,128)(2,1)} %reshape.117) | data formatting | bytes 5242880
  208.8 2.9 %copy.34 = bf16[32,32,1,1280]{3,1,2,0:T(8,128)(2,1)} copy(bf16[32,32,1,1280]{3,0,1,2:T(8,128)(2,1)S(1)} %bitcast.62) | data formatting | bytes 5242880 | tf_op jit(solution)/shard_map/all_to_all | solution.py:99
  (18 shorter events, 0.9 us)
Async XLA Ops:
  1.0 6.0 %collective-permute-start.1 = (bf16[34,4,4,128]{3,2,1,0:T(4,128)(2,1)S(1)}, bf16[34,4,4,128]{3,2,1,0:T(4,128)(2,1)S(1)}, u32[]{:S(2)}, u32[]{:S(2)}) collective-permute-start(bf16[34,4,4,128]{3,2,1,0:T(4,128)(2,1)S(1)} %pad_maximum_fusion.1), channel_id=1, source_target_pairs={{2,0},{4,2},{6,4},{0,6},{3,1},{5,3},{7,5},{1,7},{10,8},{12,10},{14... | collective-permute-start | bytes 417800 | tf_op jit(solution)/shard_map/ppermute | solution.py:18
  4.1 6.3 %collective-permute-start = (bf16[34,4,4,128]{3,2,1,0:T(4,128)(2,1)S(1)}, bf16[34,4,4,128]{3,2,1,0:T(4,128)(2,1)S(1)}, u32[]{:S(2)}, u32[]{:S(2)}) collective-permute-start(bf16[34,4,4,128]{3,2,1,0:T(4,128)(2,1)S(1)} %pad_maximum_fusion.1), channel_id=1, source_target_pairs={{0,2},{2,4},{4,6},{6,0},{1,3},{3,5},{5,7},{7,1},{8,10},{10,12},{12... | collective-permute-start | bytes 417800 | tf_op jit(solution)/shard_map/ppermute | solution.py:15
  16.1 37.6 %all-to-all-start = ((bf16[32,32,512]{2,0,1:T(8,128)(2,1)}), bf16[32,32,512]{2,0,1:T(8,128)(2,1)S(1)}, u32[]{:S(2)}, u32[]{:S(2)}) async-start(bf16[32,32,512]{2,0,1:T(8,128)(2,1)} %copy.35), calls=%async_computation | async-start | bytes 2097152 | tf_op jit(solution)/shard_map/all_to_all | solution.py:77
  53.6 6.9 %copy-start.1 = (f32[1,1,4]{2,1,0:T(1,128)S(1)}, f32[1,1,4]{2,1,0:T(1,128)}, u32[]{:S(2)}) copy-start(f32[1,1,4]{2,1,0:T(1,128)} %param.12) | copy-start | bytes 52
  53.6 65.7 %all-to-all-start.1 = ((bf16[32,32,1280]{2,0,1:T(8,128)(2,1)}), bf16[32,32,1280]{2,0,1:T(8,128)(2,1)}, u32[]{:S(2)}, u32[]{:S(2)}) async-start(bf16[32,32,1280]{2,0,1:T(8,128)(2,1)} %bitcast.59), calls=%async_computation.1 | async-start | bytes 5242880 | tf_op jit(solution)/shard_map/all_to_all | solution.py:95
  68.6 1.3 copy-start
where the time goes:
time: 212 us
  blocking collectives  66.1 us (31%)
  waiting for transfers between devices  64.1 us (30%)
  local copies, waits for them, and re-layouts  26.3 us (12%)
  matrix products  22.7 us (11%)
  starting transfers between devices  20.6 us (10%)
  other arithmetic  10.5 us (5%)
    all_to_all x1, blocking collectives, on_device(): lax.all_to_all(analysis_own, 'mem', split_axis=0, concat_axis=1, tiled=True)  66.1 us
    all_to_all x1, waiting for transfers between devices, on_device(): lax.all_to_all(flat_state, 'mem', split_axis=1, concat_axis=0, tiled=True)  37 us
    all_to_all x1, waiting for transfers between devices, on_device(): lax.all_to_all(ens_part, 'mem', split_axis=1, concat_axis=0, tiled=True)  21.7 us
    unnamed x8, local copies, waits for them, and re-layouts  18.3 us
    all_to_all x1, starting transfers between devices, on_device(): lax.all_to_all(ens_part, 'mem', split_axis=1, concat_axis=0, tiled=True)  11.2 us
    dot_general x1, matrix products, inverse_root(): return jnp.dot(half_low, lower_iter, preferred_element_type=jnp.float32)  7.36 us
    all_to_all x1, starting transfers between devices, on_device(): lax.all_to_all(flat_state, 'mem', split_axis=1, concat_axis=0, tiled=True)  6.28 us
    dot_general x1, matrix products, on_device(): jnp.einsum('pkj,kps->jps', weight_stack, state_full, preferred_element_ty...  6.13 us
  transfers between devices with their start and end apart: 4, of which 4 were waited for; matrix products, arithmetic and copies ran while one was open for 12% of the time, Pallas kernels for 0%

commit v1 on v0

--- a/solution.py
+++ b/solution.py
@@ -96,7 +96,12 @@
     analysis_own = jnp.einsum(
         "pkj,kps->jps", weight_stack, state_full, preferred_element_type=jnp.float32
     ).astype(jnp.bfloat16)
-    returned = lax.all_to_all(analysis_own, "mem", split_axis=0, concat_axis=1, tiled=True)
+    returned = jnp.concatenate(
+        lax.all_to_all(
+            jnp.stack(jnp.split(analysis_own, lax.axis_size("mem"), axis=0)), "mem", 0, 0
+        ),
+        axis=1,
+    )
     return returned.reshape(local_members, group_patches, 1, state_len)
 
 

time: 212 us -> 194 us (0.915)
  local copies, waits for them, and re-layouts: 26.3 us -> 13.7 us
  other arithmetic: 10.5 us -> 6.08 us
    unnamed x8 -> x36, local copies, waits for them, and re-layouts: 18.3 us -> 6.23 us
    convert_element_type x1 -> x0, other arithmetic: 4.42 us -> none  [on_device(): analysis_own = jnp.einsum('pkj,kps->jps', weight_stack, state_full, prefe...]
    all_to_all x1 -> x0, local copies, waits for them, and re-layouts: 2.93 us -> none  [on_device(): lax.all_to_all(analysis_own, 'mem', split_axis=0, concat_axis=1, tiled=True)]
    reshape x0 -> x1, local copies, waits for them, and re-layouts: none -> 2.93 us  [on_device(): jnp.concatenate(lax.all_to_all(jnp.stack(jnp.split(analysis_own, lax.axis...]
  transfers between devices with their start and end apart: 4 -> 4, of which waited for: 4 -> 4; matrix products, arithmetic and copies ran while one was open for 12% -> 13% of each run, Pallas kernels for 0% -> 0%
where the time goes in v1:
time: 194 us
  blocking collectives  65.9 us (34%)
  waiting for transfers between devices  64 us (33%)
  matrix products  21.7 us (11%)
  starting transfers between devices  20.6 us (11%)
  local copies, waits for them, and re-layouts  13.7 us (7%)
  other arithmetic  6.08 us (3%)
    all_to_all x1, blocking collectives, on_device(): lax.all_to_all(jnp.stack(jnp.split(analysis_own, lax.axis_size('mem'), ax...  65.9 us
    all_to_all x1, waiting for transfers between devices, on_device(): lax.all_to_all(flat_state, 'mem', split_axis=1, concat_axis=0, tiled=True)  36.8 us
    all_to_all x1, waiting for transfers between devices, on_device(): lax.all_to_all(ens_part, 'mem', split_axis=1, concat_axis=0, tiled=True)  21.7 us
    all_to_all x1, starting transfers between devices, on_device(): lax.all_to_all(ens_part, 'mem', split_axis=1, concat_axis=0, tiled=True)  11.2 us
    dot_general x1, matrix products, inverse_root(): return jnp.dot(half_low, lower_iter, preferred_element_type=jnp.float32)  7.36 us
    all_to_all x1, starting transfers between devices, on_device(): lax.all_to_all(flat_state, 'mem', split_axis=1, concat_axis=0, tiled=True)  6.28 us
    unnamed x36, local copies, waits for them, and re-layouts  6.23 us
    dot_general x1, matrix products, on_device(): jnp.einsum('pkj,kps->jps', weight_stack, state_full, preferred_element_ty...  5.09 us
  transfers between devices with their start and end apart: 4, of which 4 were waited for; matrix products, arithmetic and copies ran while one was open for 13% of the time, Pallas kernels for 0%

profile of v1, /device:TPU:32, one launch (start us, length us, event | category | flops | bytes accessed | tf_op | source)
XLA Modules:
  0.0 193.7 jit_solution(11152632563793393357)
XLA Ops:
  0.0 1.0 pad_maximum_fusion.1
  1.0 3.1 %collective-permute-start.1 = (bf16[34,4,4,128]{3,2,1,0:T(4,128)(2,1)S(1)}, bf16[34,4,4,128]{3,2,1,0:T(4,128)(2,1)S(1)}, u32[]{:S(2)}, u32[]{:S(2)}) collective-permute-start(bf16[34,4,4,128]{3,2,1,0:T(4,128)(2,1)S(1)} %pad_maximum_fusion.1), channel_id=1, source_target_pairs={{2,0},{4,2},{6,4},{0,6},{3,1},{5,3},{7,5},{1,7},{10,8},{12,10},{14... | collective-permute-start | bytes 417800 | tf_op jit(solution)/shard_map/ppermute | solution.py:18
  4.1 0.7 compare_select_fusion
  4.8 0.1 copy.16
  4.9 0.1 reshape.104
  5.0 2.0 %collective-permute-done.1 = bf16[34,4,4,128]{3,2,1,0:T(4,128)(2,1)S(1)} collective-permute-done((bf16[34,4,4,128]{3,2,1,0:T(4,128)(2,1)S(1)}, bf16[34,4,4,128]{3,2,1,0:T(4,128)(2,1)S(1)}, u32[]{:S(2)}, u32[]{:S(2)}) %collective-permute-start.1) | collective-permute-done | bytes 139296 | tf_op jit(solution)/shard_map/ppermute | solution.py:18
  7.1 3.4 %collective-permute-done = bf16[34,4,4,128]{3,2,1,0:T(4,128)(2,1)S(1)} collective-permute-done((bf16[34,4,4,128]{3,2,1,0:T(4,128)(2,1)S(1)}, bf16[34,4,4,128]{3,2,1,0:T(4,128)(2,1)S(1)}, u32[]{:S(2)}, u32[]{:S(2)}) %collective-permute-start) | collective-permute-done | bytes 139296 | tf_op jit(solution)/shard_map/ppermute | solution.py:15
  10.5 1.2 pad_maximum_fusion
  11.7 0.3 copy.15
  12.0 0.8 gather_fusion
  12.8 0.6 copy.25
  13.4 0.6 slice.22
  14.1 0.4 reshape.117
  14.5 1.6 copy.21
  16.1 11.2 %all-to-all-start = ((bf16[32,32,512]{2,0,1:T(8,128)(2,1)}), bf16[32,32,512]{2,0,1:T(8,128)(2,1)S(1)}, u32[]{:S(2)}, u32[]{:S(2)}) async-start(bf16[32,32,512]{2,0,1:T(8,128)(2,1)} %copy.21), calls=%async_computation | async-start | bytes 2097152 | tf_op jit(solution)/shard_map/all_to_all | solution.py:77
  27.3 4.7 %copy.24 = bf16[32,32,1,1280]{3,0,1,2:T(8,128)(2,1)} copy(bf16[32,32,1,1280]{3,1,2,0:T(8,128)(2,1)} %param.13) | data formatting | bytes 5242880 | tf_op args[6]
  31.9 21.7 %all-to-all-done = bf16[32,32,512]{2,0,1:T(8,128)(2,1)S(1)} async-done(((bf16[32,32,512]{2,0,1:T(8,128)(2,1)}), bf16[32,32,512]{2,0,1:T(8,128)(2,1)S(1)}, u32[]{:S(2)}, u32[]{:S(2)}) %all-to-all-start) | async-done | bytes 1048608 | tf_op jit(solution)/shard_map/all_to_all | solution.py:77
  53.6 6.3 %all-to-all-start.1 = ((bf16[32,32,1280]{2,0,1:T(8,128)(2,1)}), bf16[32,32,1280]{2,0,1:T(8,128)(2,1)}, u32[]{:S(2)}, u32[]{:S(2)}) async-start(bf16[32,32,1280]{2,0,1:T(8,128)(2,1)} %bitcast.185), calls=%async_computation.1 | async-start | bytes 5242880 | tf_op jit(solution)/shard_map/all_to_all | solution.py:95
  60.6 0.1 convert_multiply_fusion
  60.7 0.2 multiply_convert_fusion
  60.9 0.4 fusion.64
  61.3 3.9 %select_reduce_fusion = (f32[]{:T(128)}, f32[1024,1024]{1,0:T(8,128)}) fusion(bf16[1024,512]{1,0:T(8,128)(2,1)S(1)} %bitcast.195, bf16[1024,512]{1,0:T(8,128)(2,1)S(1)} %bitcast.193), kind=kOutput, calls=%fused_computation.10 | convolution fusion | flops 1080033280 | bytes 6291460 | tf_op jit(solution)/shard_map/while/body/eval_jaxpr/dot_general | solution.py:85
  65.9 2.8 %divide_convert_fusion.1 = bf16[1024,1024]{1,0:T(8,128)(2,1)S(1)} fusion(f32[1024,1024]{1,0:T(8,128)} %get-tuple-element.16, f32[]{:T(128)S(6)} %div.29), kind=kLoop, calls=%fused_computation.9 | loop fusion | flops 6291456 | bytes 6291460 | tf_op jit(solution)/shard_map/while/body/eval_jaxpr/convert_element_type | solution.py:50
  68.7 1.3 copy-done
  70.0 3.7 %fusion.21 = bf16[1024,1024]{1,0:T(8,128)(2,1)} fusion(bf16[1024,1024]{1,0:T(8,128)(2,1)S(1)} %divide_convert_fusion.1), kind=kOutput, calls=%fused_computation.24 | convolution fusion | flops 2153775104 | bytes 4194304 | tf_op jit(solution)/shard_map/while/body/eval_jaxpr/dot_general | solution.py:37
  73.8 7.4 %divide_convert_fusion = bf16[1024,1024]{1,0:T(8,128)(2,1)S(1)} fusion(f32[]{:T(128)S(6)} %sqrt.4, bf16[1024,1024]{1,0:T(8,128)(2,1)} %fusion.21, bf16[1024,1024]{1,0:T(8,128)(2,1)} %copy-done), kind=kOutput, calls=%fused_computation.8 | convolution fusion | flops 4314890240 | bytes 6291460 | tf_op jit(solution)/shard_map/while/body/eval_jaxpr/dot_general | solution.py:36
  81.1 0.6 fusion.65
  81.8 0.6 fusion.66
  82.4 36.8 %all-to-all-done.1 = bf16[32,32,1280]{2,0,1:T(8,128)(2,1)} async-done(((bf16[32,32,1280]{2,0,1:T(8,128)(2,1)}), bf16[32,32,1280]{2,0,1:T(8,128)(2,1)}, u32[]{:S(2)}, u32[]{:S(2)}) %all-to-all-start.1) | async-done | bytes 2621472 | tf_op jit(solution)/shard_map/all_to_all | solution.py:95
  119.3 5.1 %fusion.4 = bf16[1024,1,1280]{2,0,1:T(8,128)(2,1)S(1)} fusion(bf16[1024,1280]{1,0:T(8,128)(2,1)} %bitcast.22, bf16[1024,1024]{1,0:T(8,128)(2,1)S(1)} %divide_convert_fusion, f32[1024]{0:T(1024)S(1)} %bitcast.202), kind=kOutput, calls=%fused_computation.14 | convolution fusion | flops 2688811008 | bytes 7344128 | tf_op jit(solution)/shard_map/pkj,kps->jps/dot_general | solution.py:96
  124.9 65.9 %all_to_all.35 = bf16[32,32,1,1280]{3,1,2,0:T(8,128)(2,1)S(1)} all-to-all(bf16[32,32,1,1280]{3,1,2,0:T(8,128)(2,1)S(1)} %fusion.23), channel_id=1, replica_groups=mesh['mem'=32,'lon'=4,'lat'=2] {'mem'}, dimensions={0} | all-to-all | bytes 5242880 | tf_op jit(solution)/shard_map/all_to_all | solution.py:100
  190.8 2.9 %copy.20 = bf16[32,32,1,1280]{3,1,2,0:T(8,128)(2,1)} copy(bf16[32,32,1,1280]{3,0,2,1:T(8,128)(2,1)S(1)} %bitcast.188) | data formatting | bytes 5242880 | tf_op jit(solution)/shard_map/reshape | solution.py:99
  (45 shorter events, 0.4 us)
Async XLA Ops:
  1.0 6.0 %collective-permute-start.1 = (bf16[34,4,4,128]{3,2,1,0:T(4,128)(2,1)S(1)}, bf16[34,4,4,128]{3,2,1,0:T(4,128)(2,1)S(1)}, u32[]{:S(2)}, u32[]{:S(2)}) collective-permute-start(bf16[34,4,4,128]{3,2,1,0:T(4,128)(2,1)S(1)} %pad_maximum_fusion.1), channel_id=1, source_target_pairs={{2,0},{4,2},{6,4},{0,6},{3,1},{5,3},{7,5},{1,7},{10,8},{12,10},{14... | collective-permute-start | bytes 417800 | tf_op jit(solution)/shard_map/ppermute | solution.py:18
  4.1 6.3 %collective-permute-start = (bf16[34,4,4,128]{3,2,1,0:T(4,128)(2,1)S(1)}, bf16[34,4,4,128]{3,2,1,0:T(4,128)(2,1)S(1)}, u32[]{:S(2)}, u32[]{:S(2)}) collective-permute-start(bf16[34,4,4,128]{3,2,1,0:T(4,128)(2,1)S(1)} %pad_maximum_fusion.1), channel_id=1, source_target_pairs={{0,2},{2,4},{4,6},{6,0},{1,3},{3,5},{5,7},{7,1},{8,10},{10,12},{12... | collective-permute-start | bytes 417800 | tf_op jit(solution)/shard_map/ppermute | solution.py:15
  16.1 37.6 %all-to-all-start = ((bf16[32,32,512]{2,0,1:T(8,128)(2,1)}), bf16[32,32,512]{2,0,1:T(8,128)(2,1)S(1)}, u32[]{:S(2)}, u32[]{:S(2)}) async-start(bf16[32,32,512]{2,0,1:T(8,128)(2,1)} %copy.21), calls=%async_computation | async-start | bytes 2097152 | tf_op jit(solution)/shard_map/all_to_all | solution.py:77
  53.6 6.9 %copy-start.1 = (f32[1,1,4]{2,1,0:T(1,128)S(1)}, f32[1,1,4]{2,1,0:T(1,128)}, u32[]{:S(2)}) copy-start(f32[1,1,4]{2,1,0:T(1,128)} %param.12) | copy-start | bytes 52
  53.6 65.7 %all-to-all-start.1 = ((bf16[32,32,1280]{2,0,1:T(8,128)(2,1)}), bf16[32,32,1280]{2,0,1:T(8,128)(2,1)}, u32[]{:S(2)}, u32[]{:S(2)}) async-start(bf16[32,32,1280]{2,0,1:T(8,128)(2,1)} %bitcast.185), calls=%async_computation.1 | async-start | bytes 5242880 | tf_op jit(solution)/shard_map/all_to_all | solution.py:95
  68.7 1.3 copy-start
